TPU v7x, 128 devices: a whole 4x4x4 slice. The times are simulated.
128 devices in a mesh: dp: 16 (over x, z_lo, core), ctx: 8 (over z_hi, y).
Axes of the slice: x: 4, y: 4, z: 4 (z_hi: 2, z_lo: 2; z = z_hi * 2 + z_lo), core: 2. Of those that a mesh axis runs over, the one named last changes fastest.
Arguments:
- document: bfloat16 [16, 2048, 1024], P('dp', 'ctx'), may hold values from -45 to 45, as said below
- summary: bfloat16 [16, 1024, 1024], P('dp', 'ctx'), may hold values from -45 to 45, as said below
- encoder_gain: float32 [1024], replicated, may hold values from 0.5 to 1.5
- query_weight: bfloat16 [1024, 1024], replicated, as said below
- key_weight: bfloat16 [1024, 1024], replicated, as said below
- value_weight: bfloat16 [1024, 1024], replicated, may hold values from -0.1875 to 0.1875
- output_weight: bfloat16 [1024, 1024], replicated, may hold values from -0.1875 to 0.1875
- memory_gain: float32 [1024], replicated, may hold values from 0.5 to 1.5
- summary_gain: float32 [1024], replicated, may hold values from 0.5 to 1.5
- cross_query: bfloat16 [1024, 1024], replicated, as said below
- cross_key: bfloat16 [1024, 1024], replicated, as said below
- cross_value: bfloat16 [1024, 1024], replicated, may hold values from -0.1875 to 0.1875
- cross_output: bfloat16 [1024, 1024], replicated, may hold values from -0.1875 to 0.1875
- encoder_cotangent: bfloat16 [16, 2048, 1024], P('dp', 'ctx'), as said below
- decoder_cotangent: bfloat16 [16, 1024, 1024], P('dp', 'ctx'), as said below
Outputs:
- encoded: bfloat16 [16, 2048, 1024], P('dp', 'ctx')
- decoded: bfloat16 [16, 1024, 1024], P('dp', 'ctx')
- output_grad: bfloat16 [1024, 1024], replicated
- cross_grad: bfloat16 [1024, 1024], replicated
Inputs may be any that keep to these rules, and one draw needn't show every extreme that they name: `document`: encoder states of order one. `summary`: decoder states of order one. `query_weight`: entries of order one over the square root of 1024. `key_weight`: entries of order one over the square root of 1024. `cross_query`: entries of order one over the square root of 1024. `cross_key`: entries of order one over the square root of 1024. `encoder_cotangent`: entries of order one over the square root of 32768. `decoder_cotangent`: entries of order one over the square root of 16384.
All inputs are finite; a program needn't handle non-finite values.
Results may differ from a plain program's by a relative error of at most 0.035.
The roundings to bfloat16 on the way count: a program that leaves them out, or rounds other values in their place, can miss the bound.
Values may be sent and summed in bfloat16 or wider, within the bound.
A program may use at most 192 MiB of HBM per device.

v0:
```python
import jax
import jax.numpy as jnp
from jax import lax
from jax.sharding import PartitionSpec as P

HEADS = 16
HEAD_DIM = 64


def norm_rows(rows, gain):
    values = rows.astype(jnp.float32)
    scale = lax.rsqrt(jnp.mean(values * values, axis=-1, keepdims=True) + 1e-06)
    return (values * scale * gain).astype(jnp.bfloat16)


def project(rows, weight):
    return jnp.dot(rows, weight, preferred_element_type=jnp.float32).astype(jnp.bfloat16)


def start_carry(count):
    best = jnp.full((HEADS, count), -jnp.inf, jnp.float32)
    total = jnp.zeros((HEADS, count), jnp.float32)
    accum = jnp.zeros((count, HEADS * HEAD_DIM), jnp.float32)
    return (best, total, accum)


def softmax_step(carry, query_heads, keys, values):
    best, total, accum = carry
    count = query_heads.shape[0]
    key_heads = keys.reshape(keys.shape[0], HEADS, HEAD_DIM)
    value_heads = values.reshape(values.shape[0], HEADS, HEAD_DIM)
    scores = jnp.einsum("qhd,khd->hqk", query_heads, key_heads, preferred_element_type=jnp.float32)
    new_best = jnp.max(scores, axis=-1)
    weights = jnp.exp(scores - new_best[:, :, None])
    decay = jnp.exp(best - new_best)
    total = total * decay + jnp.sum(weights, axis=-1)
    mixed = jnp.einsum(
        "hqk,khd->qhd",
        weights.astype(jnp.bfloat16),
        value_heads,
        preferred_element_type=jnp.float32,
    )
    accum = accum * jnp.repeat(jnp.transpose(decay), HEAD_DIM, axis=1) + mixed.reshape(
        count, HEADS * HEAD_DIM
    )
    return (new_best, total, accum)


def finish(carry):
    best, total, accum = carry
    return (accum / jnp.repeat(jnp.transpose(total), HEAD_DIM, axis=1)).astype(jnp.bfloat16)


def row_products(left, right):
    return lax.dot_general(
        left, right, (((0,), (0,)), ((), ())), preferred_element_type=jnp.float32
    )


def body(
    document,
    summary,
    encoder_gain,
    query_weight,
    key_weight,
    value_weight,
    output_weight,
    memory_gain,
    summary_gain,
    cross_query,
    cross_key,
    cross_value,
    cross_output,
    encoder_cotangent,
    decoder_cotangent,
):
    rows = document[0]
    states = summary[0]
    normed = norm_rows(rows, encoder_gain)
    query = project(normed, query_weight)
    keys = project(normed, key_weight)
    values = project(normed, value_weight)
    query_heads = query.reshape(rows.shape[0], HEADS, HEAD_DIM)
    piece = (
        lax.all_gather(keys, "ctx", axis=0, tiled=True),
        lax.all_gather(values, "ctx", axis=0, tiled=True),
    )
    heads = finish(softmax_step(start_carry(rows.shape[0]), query_heads, piece[0], piece[1]))
    own_local = row_products(heads, encoder_cotangent[0])
    encoded = (
        rows.astype(jnp.float32) + jnp.dot(heads, output_weight, preferred_element_type=jnp.float32)
    ).astype(jnp.bfloat16)
    memory = norm_rows(encoded, memory_gain)
    summary_query = project(norm_rows(states, summary_gain), cross_query)
    summary_heads = summary_query.reshape(states.shape[0], HEADS, HEAD_DIM)
    memory_keys = project(memory, cross_key)
    memory_values = project(memory, cross_value)
    piece = (
        lax.all_gather(memory_keys, "ctx", axis=0, tiled=True),
        lax.all_gather(memory_values, "ctx", axis=0, tiled=True),
    )
    folded = softmax_step(start_carry(states.shape[0]), summary_heads, piece[0], piece[1])
    cross_heads = finish(folded)
    decoded = (
        states.astype(jnp.float32)
        + jnp.dot(cross_heads, cross_output, preferred_element_type=jnp.float32)
    ).astype(jnp.bfloat16)
    cross_local = row_products(cross_heads, decoder_cotangent[0])
    own_sum, cross_sum = lax.psum((own_local, cross_local), ("dp", "ctx"))
    return (
        encoded[None],
        decoded[None],
        own_sum.astype(jnp.bfloat16),
        cross_sum.astype(jnp.bfloat16),
    )


def solution(mesh):
    in_specs = (
        P("dp", "ctx", None),
        P("dp", "ctx", None),
        P(),
        P(),
        P(),
        P(),
        P(),
        P(),
        P(),
        P(),
        P(),
        P(),
        P(),
        P("dp", "ctx", None),
        P("dp", "ctx", None),
    )
    out_specs = (P("dp", "ctx", None), P("dp", "ctx", None), P(), P())
    return jax.shard_map(body, mesh=mesh, in_specs=in_specs, out_specs=out_specs, check_vma=False)
```

profile of v0, /device:TPU:0, one launch (start us, length us, event | category | flops | bytes accessed | tf_op | source)
XLA Modules:
  0.0 466.5 jit_solution(679255280130076172)
XLA Ops:
  7.2 0.0 copy-start
  7.2 0.0 copy-start.5
  7.2 0.0 copy-start.9
  7.2 0.0 all-gather.5.cloned.1.call-start
  7.3 1.4 fusion.34
  8.6 3.3 convolution_convert_fusion.3
  12.0 0.0 all-gather.5.cloned.1.call-update
  12.0 0.0 all-gather.7.cloned.1.call-start
  12.1 0.0 copy-done.5
  12.1 0.0 copy-done.9
  12.1 3.1 convolution_convert_fusion.2
  15.2 0.0 all-gather.7.cloned.1.call-update
  15.2 0.0 all-gather.9.cloned.1.call-start
  15.3 3.1 convolution_convert_fusion.4
  18.4 1.2 copy.25
  19.7 66.6 %all-gather.5.cloned.1.call-done = bf16[2048,1024]{1,0:T(8,128)(2,1)} async-done(((bf16[256,1024]{1,0:T(8,128)(2,1)}), bf16[2048,1024]{1,0:T(8,128)(2,1)}) %all-gather.5.cloned.1.call-update) | async-done | bytes 4194320 | tf_op jit(solution)/shard_map/all_gather | solution.py:85
  86.3 6.5 %copy.26 = bf16[2048,1024]{0,1:T(8,128)(2,1)} copy(bf16[2048,1024]{1,0:T(8,128)(2,1)} %all-gather.5.cloned.1.call-done) | data formatting | bytes 8388608 | tf_op jit(solution)/shard_map/all_gather | solution.py:85
  92.8 15.5 %fusion.59 = (f32[16,256]{1,0:T(8,128)S(1)}, f32[16,256,2048]{2,1,0:T(8,128)}) fusion(bf16[256,16,64]{0,2,1:T(8,128)(2,1)S(1)} %bitcast.85, bf16[2048,16,64]{0,2,1:T(8,128)(2,1)} %bitcast.80), kind=kOutput, calls=%fused_computation.58 | convolution fusion | flops 1082126336 | bytes 38289408 | tf_op jit(solution)/shard_map/qhd,khd->hqk/dot_general | solution.py:32
  108.3 13.6 %fusion = f32[16,256]{1,0:T(8,128)S(1)} fusion(f32[16,256,2048]{2,1,0:T(8,128)} %get-tuple-element.7, f32[16,256]{1,0:T(8,128)S(1)} %get-tuple-element.6), kind=kLoop, calls=%fused_computation.1 | loop fusion | flops 16773120 | bytes 33587200 | tf_op jit(solution)/shard_map/reduce_sum | solution.py:36
  121.9 36.6 %all-gather.7.cloned.1.call-done = bf16[2048,1024]{1,0:T(8,128)(2,1)} async-done(((bf16[256,1024]{1,0:T(8,128)(2,1)}), bf16[2048,1024]{1,0:T(8,128)(2,1)}) %all-gather.7.cloned.1.call-update) | async-done | bytes 4194320 | tf_op jit(solution)/shard_map/all_gather | solution.py:86
  158.6 6.5 %copy.27 = bf16[2048,1024]{0,1:T(8,128)(2,1)} copy(bf16[2048,1024]{1,0:T(8,128)(2,1)} %all-gather.7.cloned.1.call-done) | data formatting | bytes 8388608 | tf_op jit(solution)/shard_map/all_gather | solution.py:86
  165.1 0.0 copy-start.10
  165.1 15.0 %fusion.27 = bf16[256,16,64]{0,2,1:T(8,128)(2,1)S(1)} fusion(bf16[2048,16,64]{0,2,1:T(8,128)(2,1)} %bitcast.81, f32[16,256,2048]{2,1,0:T(8,128)} %get-tuple-element.7, f32[16,256]{1,0:T(8,128)S(1)} %get-tuple-element.6, f32[256,16]{0,1:T(8,128)S(1)} %bitcast_add_fusion, f32[256,16]{0,1:T(8,128)S(1)} %multiply_bitcast_fusion), kind=kOutput, calls=%fused_computation.29 | convolution fusion | flops 1091305472 | bytes 38322176 | tf_op jit(solution)/shard_map/hqk,khd->qhd/dot_general | solution.py:37
  180.1 0.0 copy-done
  180.1 0.8 fusion.31
  180.9 0.0 copy-start.6
  181.0 0.8 copy-done.6
  181.7 0.0 copy-done.10
  181.7 0.0 copy-start.2
  181.7 0.0 copy-start.3
  181.7 0.0 copy-start.8
  181.8 3.3 convolution_convert_fusion.1
  185.0 0.0 all-gather.9.cloned.1.call-update
  185.1 0.2 all-gather.11.cloned.1.call-start
  185.3 3.3 convolution_convert_fusion
  188.6 0.0 all-gather.11.cloned.1.call-update
  188.7 0.0 copy-done.2
  188.7 0.1 fusion.43
  188.8 0.0 copy-done.3
  188.8 0.0 copy-done.8
  188.8 0.5 convolution_convert_fusion.5
  189.3 0.2 copy.28
  189.5 3.7 fusion.46
  193.2 61.4 %all-gather.9.cloned.1.call-done = bf16[2048,1024]{1,0:T(8,128)(2,1)} async-done(((bf16[256,1024]{1,0:T(8,128)(2,1)}), bf16[2048,1024]{1,0:T(8,128)(2,1)}) %all-gather.9.cloned.1.call-update) | async-done | bytes 4194320 | tf_op jit(solution)/shard_map/all_gather | solution.py:99
  254.6 6.4 %copy.29 = bf16[2048,1024]{0,1:T(8,128)(2,1)} copy(bf16[2048,1024]{1,0:T(8,128)(2,1)} %all-gather.9.cloned.1.call-done) | data formatting | bytes 8388608 | tf_op jit(solution)/shard_map/all_gather | solution.py:99
  261.0 10.3 %fusion.60 = (f32[16,128]{1,0:T(8,128)S(1)}, f32[16,128,2048]{2,1,0:T(8,128)}) fusion(bf16[128,16,64]{0,2,1:T(8,128)(2,1)S(1)} %bitcast.88, bf16[2048,16,64]{0,2,1:T(8,128)(2,1)} %bitcast.79), kind=kOutput, calls=%fused_computation.59 | convolution fusion | flops 541063168 | bytes 21241856 | tf_op jit(solution)/shard_map/qhd,khd->hqk/dot_general | solution.py:32
  271.3 8.2 %fusion.5 = f32[16,128]{1,0:T(8,128)S(1)} fusion(f32[16,128,2048]{2,1,0:T(8,128)} %get-tuple-element.11, f32[16,128]{1,0:T(8,128)S(1)} %get-tuple-element.10), kind=kLoop, calls=%fused_computation.6 | loop fusion | flops 8386560 | bytes 16793600 | tf_op jit(solution)/shard_map/reduce_sum | solution.py:36
  279.6 47.1 %all-gather.11.cloned.1.call-done = bf16[2048,1024]{1,0:T(8,128)(2,1)} async-done(((bf16[256,1024]{1,0:T(8,128)(2,1)}), bf16[2048,1024]{1,0:T(8,128)(2,1)}) %all-gather.11.cloned.1.call-update) | async-done | bytes 4194320 | tf_op jit(solution)/shard_map/all_gather | solution.py:100
  326.7 6.4 %copy.30 = bf16[2048,1024]{0,1:T(8,128)(2,1)} copy(bf16[2048,1024]{1,0:T(8,128)(2,1)} %all-gather.11.cloned.1.call-done) | data formatting | bytes 8388608 | tf_op jit(solution)/shard_map/all_gather | solution.py:100
  333.1 0.0 copy-start.7
  333.1 10.2 %fusion.40 = bf16[128,16,64]{0,2,1:T(8,128)(2,1)S(1)} fusion(bf16[2048,16,64]{0,2,1:T(8,128)(2,1)} %bitcast.82, f32[16,128,2048]{2,1,0:T(8,128)} %get-tuple-element.11, f32[16,128]{1,0:T(8,128)S(1)} %get-tuple-element.10, f32[128,16]{0,1:T(8,128)S(1)} %bitcast_add_fusion.1, f32[128,16]{0,1:T(8,128)S(1)} %multiply_bitcast_fusion.1), kind=kOutput, calls=%fused_computation.38 | convolution fusion | flops 545652736 | bytes 21258240 | tf_op jit(solution)/shard_map/hqk,khd->qhd/dot_general | solution.py:37
  343.4 0.0 copy-start.4
  343.4 0.0 copy-done.7
  343.4 2.6 fusion.49
  346.0 0.0 copy-done.4
  346.0 0.0 copy-start.1
  346.1 1.2 fusion.30
  347.2 112.7 %all-reduce.2 = (bf16[1024,1024]{1,0:T(8,128)(2,1)}, bf16[1024,1024]{1,0:T(8,128)(2,1)}) all-reduce(f32[1024,1024]{1,0:T(8,128)} %fusion.46, f32[1024,1024]{1,0:T(8,128)} %fusion.49), channel_id=1, replica_groups=mesh['dp'=16,'ctx'=8] {'dp','ctx'}, use_global_device_ids=true, to_apply=%region_7.0 | all-reduce | flops 2097152 | bytes 12582912 | tf_op jit(solution)/shard_map/psum | solution.py:109
  459.9 0.0 copy-done.1
  (7 shorter events, 0.1 us)
Async XLA Ops:
  7.2 172.9 %copy-start = (bf16[1024,1024]{1,0:T(8,128)(2,1)S(1)}, bf16[1024,1024]{1,0:T(8,128)(2,1)}, u32[]{:S(2)}) copy-start(bf16[1024,1024]{1,0:T(8,128)(2,1)} %param.21) | copy-start | bytes 6291460
  7.2 4.9 %copy-start.5 = (bf16[1,256,1024]{2,1,0:T(8,128)(2,1)S(1)}, bf16[1,256,1024]{2,1,0:T(8,128)(2,1)}, u32[]{:S(2)}) copy-start(bf16[1,256,1024]{2,1,0:T(8,128)(2,1)} %param.15) | copy-start | bytes 1572868
  7.2 4.9 %copy-start.9 = (f32[1024]{0:T(1024)S(1)}, f32[1024]{0:T(1024)}, u32[]{:S(2)}) copy-start(f32[1024]{0:T(1024)} %param.17) | copy-start | bytes 12292
  7.2 79.1 %all-gather.5.cloned.1.call-start = ((), (), s32[]{:S(2)}) async-start(), calls=%async_computation | async-start | bytes 4718592 | tf_op jit(solution)/shard_map/all_gather | solution.py:85
  12.0 146.6 %all-gather.7.cloned.1.call-start = ((), (), s32[]{:S(2)}) async-start(), calls=%async_computation.1 | async-start | bytes 4718592 | tf_op jit(solution)/shard_map/all_gather | solution.py:86
  15.2 239.3 %all-gather.9.cloned.1.call-start = ((), (), s32[]{:S(2)}) async-start(), calls=%async_computation.2 | async-start | bytes 4718592 | tf_op jit(solution)/shard_map/all_gather | solution.py:99
  165.1 16.7 %copy-start.10 = (f32[1024]{0:T(1024)S(1)}, f32[1024]{0:T(1024)}, u32[]{:S(2)}) copy-start(f32[1024]{0:T(1024)} %param.22) | copy-start | bytes 12292
  180.9 0.8 copy-start.6
  181.7 6.9 %copy-start.2 = (bf16[1,128,1024]{2,1,0:T(8,128)(2,1)S(1)}, bf16[1,128,1024]{2,1,0:T(8,128)(2,1)}, u32[]{:S(2)}) copy-start(bf16[1,128,1024]{2,1,0:T(8,128)(2,1)} %param.16) | copy-start | bytes 786436
  181.7 7.1 %copy-start.3 = (bf16[1024,1024]{1,0:T(8,128)(2,1)S(1)}, bf16[1024,1024]{1,0:T(8,128)(2,1)}, u32[]{:S(2)}) copy-start(bf16[1024,1024]{1,0:T(8,128)(2,1)} %param.24) | copy-start | bytes 6291460
  181.7 7.1 %copy-start.8 = (f32[1024]{0:T(1024)S(1)}, f32[1024]{0:T(1024)}, u32[]{:S(2)}) copy-start(f32[1024]{0:T(1024)} %param.23) | copy-start | bytes 12292
  185.1 141.6 %all-gather.11.cloned.1.call-start = ((), (), s32[]{:S(2)}) async-start(), calls=%async_computation.3 | async-start | bytes 4718592 | tf_op jit(solution)/shard_map/all_gather | solution.py:100
  333.1 10.3 %copy-start.7 = (bf16[1,128,1024]{2,1,0:T(8,128)(2,1)S(1)}, bf16[1,128,1024]{2,1,0:T(8,128)(2,1)}, u32[]{:S(2)}) copy-start(bf16[1,128,1024]{2,1,0:T(8,128)(2,1)} %param.29) | copy-start | bytes 786436
  343.4 2.7 copy-start.4
  346.0 113.9 %copy-start.1 = (bf16[1024,1024]{1,0:T(8,128)(2,1)S(1)}, bf16[1024,1024]{1,0:T(8,128)(2,1)}, u32[]{:S(2)}) copy-start(bf16[1024,1024]{1,0:T(8,128)(2,1)} %param.21) | copy-start | bytes 6291460
Sparse Core Ops, SparseCore 0:
  12.1 74.0 all-gather.4
  89.2 69.3 all-gather.6
  185.2 69.3 all-gather.8
  257.3 69.3 all-gather.10
where the time goes:
time: 468 us; the launch traced here: 466 us
  waiting for transfers between devices  212 us (45%)
  blocking collectives  113 us (24%)
  matrix products  76.2 us (16%)
  local copies, waits for them, and re-layouts  28.1 us (6%)
  other arithmetic  23.4 us (5%)
  between operations  13.9 us (3%)
    psum x1, blocking collectives, body(): own_sum, cross_sum = lax.psum((own_local, cross_local), ('dp', 'ctx'))  113 us
    all_gather x1, waiting for transfers between devices, body(): lax.all_gather(keys, 'ctx', axis=0, tiled=True)  66.6 us
    all_gather x1, waiting for transfers between devices, body(): lax.all_gather(memory_keys, 'ctx', axis=0, tiled=True)  61.4 us
    all_gather x1, waiting for transfers between devices, body(): lax.all_gather(memory_values, 'ctx', axis=0, tiled=True)  47.1 us
    all_gather x1, waiting for transfers between devices, body(): lax.all_gather(values, 'ctx', axis=0, tiled=True)  36.6 us
    dot_general x2, matrix products, softmax_step(): jnp.einsum('qhd,khd->hqk', query_heads, key_heads, preferred_element_type...  25.8 us
    dot_general x2, matrix products, softmax_step(): jnp.einsum('hqk,khd->qhd', weights.astype(jnp.bfloat16), value_heads, pre...  25.3 us
    reduce_sum x2, other arithmetic, softmax_step(): total = total * decay + jnp.sum(weights, axis=-1)  21.9 us
  transfers between devices with their start and end apart: 4, of which 4 were waited for; matrix products, arithmetic and copies ran while one was open for 16% of the time, Pallas kernels for 0%

commit v1 on v0

--- a/solution.py
+++ b/solution.py
@@ -106,7 +106,7 @@
         + jnp.dot(cross_heads, cross_output, preferred_element_type=jnp.float32)
     ).astype(jnp.bfloat16)
     cross_local = row_products(cross_heads, decoder_cotangent[0])
-    own_sum, cross_sum = lax.psum((own_local, cross_local), ("dp", "ctx"))
+    own_sum, cross_sum = lax.psum(lax.psum((own_local, cross_local), "dp"), "ctx")
     return (
         encoded[None],
         decoded[None],

time: 468 us -> 722 us (1.54)
  waiting for transfers between devices: 212 us -> 400 us
  blocking collectives: 113 us -> 176 us
    psum x0 -> x1, waiting for transfers between devices: none -> 189 us  [body(): lax.psum((own_local, cross_local), 'dp')]
    psum x1, blocking collectives: 113 us -> 176 us  [body(): lax.psum(lax.psum((own_local, cross_local), 'dp'), 'ctx')]
  transfers between devices with their start and end apart: 4 -> 5, of which waited for: 4 -> 5; matrix products, arithmetic and copies ran while one was open for 16% -> 11% of each run, Pallas kernels for 0% -> 0%
where the time goes in v1:
time: 722 us; the launch traced here: 720 us
  waiting for transfers between devices  400 us (55%)
  blocking collectives  176 us (24%)
  matrix products  78.2 us (11%)
  local copies, waits for them, and re-layouts  28.2 us (4%)
  other arithmetic  23.4 us (3%)
  between operations  13.9 us (2%)
    psum x1, waiting for transfers between devices, body(): lax.psum((own_local, cross_local), 'dp')  189 us
    psum x1, blocking collectives, body(): lax.psum(lax.psum((own_local, cross_local), 'dp'), 'ctx')  176 us
    all_gather x1, waiting for transfers between devices, body(): lax.all_gather(keys, 'ctx', axis=0, tiled=True)  66.6 us
    all_gather x1, waiting for transfers between devices, body(): lax.all_gather(memory_keys, 'ctx', axis=0, tiled=True)  60.7 us
    all_gather x1, waiting for transfers between devices, body(): lax.all_gather(memory_values, 'ctx', axis=0, tiled=True)  47.1 us
    all_gather x1, waiting for transfers between devices, body(): lax.all_gather(values, 'ctx', axis=0, tiled=True)  36.6 us
    dot_general x2, matrix products, softmax_step(): jnp.einsum('qhd,khd->hqk', query_heads, key_heads, preferred_element_type...  25.8 us
    dot_general x2, matrix products, softmax_step(): jnp.einsum('hqk,khd->qhd', weights.astype(jnp.bfloat16), value_heads, pre...  25.3 us
  transfers between devices with their start and end apart: 5, of which 5 were waited for; matrix products, arithmetic and copies ran while one was open for 11% of the time, Pallas kernels for 0%

profile of v1, /device:TPU:0, one launch (start us, length us, event | category | flops | bytes accessed | tf_op | source)
XLA Modules:
  0.0 720.3 jit_solution(3532075819449616958)
XLA Ops:
  7.2 0.0 copy-start
  7.2 0.0 copy-start.3
  7.2 0.0 copy-start.8
  7.2 0.0 all-gather.5.cloned.1.call-start
  7.3 1.4 fusion.34
  8.6 3.3 convolution_convert_fusion.3
  12.0 0.0 all-gather.5.cloned.1.call-update
  12.0 0.0 all-gather.7.cloned.1.call-start
  12.1 0.0 copy-done.3
  12.1 0.0 copy-done.8
  12.1 3.1 convolution_convert_fusion.2
  15.2 0.0 all-gather.7.cloned.1.call-update
  15.2 0.0 all-gather.9.cloned.1.call-start
  15.3 3.1 convolution_convert_fusion.4
  18.4 1.2 copy.25
  19.7 66.6 %all-gather.5.cloned.1.call-done = bf16[2048,1024]{1,0:T(8,128)(2,1)} async-done(((bf16[256,1024]{1,0:T(8,128)(2,1)}), bf16[2048,1024]{1,0:T(8,128)(2,1)}) %all-gather.5.cloned.1.call-update) | async-done | bytes 4194320 | tf_op jit(solution)/shard_map/all_gather | solution.py:85
  86.3 6.5 copy.26
  92.7 15.5 %fusion.59 = (f32[16,256]{1,0:T(8,128)S(1)}, f32[16,256,2048]{2,1,0:T(8,128)}) fusion(bf16[256,16,64]{0,2,1:T(8,128)(2,1)S(1)} %bitcast.85, bf16[2048,16,64]{0,2,1:T(8,128)(2,1)} %bitcast.80), kind=kOutput, calls=%fused_computation.58 | convolution fusion | flops 1082126336 | bytes 38289408 | tf_op jit(solution)/shard_map/qhd,khd->hqk/dot_general | solution.py:32
  108.3 13.6 %fusion = f32[16,256]{1,0:T(8,128)S(1)} fusion(f32[16,256,2048]{2,1,0:T(8,128)} %get-tuple-element.9, f32[16,256]{1,0:T(8,128)S(1)} %get-tuple-element.8), kind=kLoop, calls=%fused_computation.1 | loop fusion | flops 16773120 | bytes 33587200 | tf_op jit(solution)/shard_map/reduce_sum | solution.py:36
  121.9 36.6 %all-gather.7.cloned.1.call-done = bf16[2048,1024]{1,0:T(8,128)(2,1)} async-done(((bf16[256,1024]{1,0:T(8,128)(2,1)}), bf16[2048,1024]{1,0:T(8,128)(2,1)}) %all-gather.7.cloned.1.call-update) | async-done | bytes 4194320 | tf_op jit(solution)/shard_map/all_gather | solution.py:86
  158.6 6.5 copy.27
  165.1 0.0 copy-start.9
  165.1 15.0 %fusion.27 = bf16[256,16,64]{0,2,1:T(8,128)(2,1)S(1)} fusion(bf16[2048,16,64]{0,2,1:T(8,128)(2,1)} %bitcast.81, f32[16,256,2048]{2,1,0:T(8,128)} %get-tuple-element.9, f32[16,256]{1,0:T(8,128)S(1)} %get-tuple-element.8, f32[256,16]{0,1:T(8,128)S(1)} %bitcast_add_fusion, f32[256,16]{0,1:T(8,128)S(1)} %multiply_bitcast_fusion), kind=kOutput, calls=%fused_computation.29 | convolution fusion | flops 1091305472 | bytes 38322176 | tf_op jit(solution)/shard_map/hqk,khd->qhd/dot_general | solution.py:37
  180.1 0.0 copy-done
  180.1 0.8 fusion.31
  180.9 0.0 copy-start.5
  181.0 0.8 copy-done.5
  181.7 0.0 copy-done.9
  181.7 0.0 copy-start.2
  181.7 0.0 copy-start.7
  181.7 3.2 convolution_convert_fusion.1
  184.9 0.0 copy-start.4
  184.9 0.0 all-gather.9.cloned.1.call-update
  185.0 0.0 all-gather.11.cloned.1.call-start
  185.0 3.4 convolution_convert_fusion
  188.4 0.0 all-gather.11.cloned.1.call-update
  188.4 0.2 all-reduce.5.cloned.1.call-start
  188.6 0.0 copy-done.2
  188.6 0.1 fusion.43
  188.8 0.0 copy-done.7
  188.8 2.1 convolution_convert_fusion.5
  190.9 0.2 copy.28
  191.0 0.0 copy-done.4
  191.1 2.6 fusion.46
  193.7 60.7 %all-gather.9.cloned.1.call-done = bf16[2048,1024]{1,0:T(8,128)(2,1)} async-done(((bf16[256,1024]{1,0:T(8,128)(2,1)}), bf16[2048,1024]{1,0:T(8,128)(2,1)}) %all-gather.9.cloned.1.call-update) | async-done | bytes 4194320 | tf_op jit(solution)/shard_map/all_gather | solution.py:99
  254.4 6.5 copy.29
  260.9 10.3 %fusion.60 = (f32[16,128]{1,0:T(8,128)S(1)}, f32[16,128,2048]{2,1,0:T(8,128)}) fusion(bf16[128,16,64]{0,2,1:T(8,128)(2,1)S(1)} %bitcast.88, bf16[2048,16,64]{0,2,1:T(8,128)(2,1)} %bitcast.79), kind=kOutput, calls=%fused_computation.59 | convolution fusion | flops 541063168 | bytes 21241856 | tf_op jit(solution)/shard_map/qhd,khd->hqk/dot_general | solution.py:32
  271.2 8.2 %fusion.5 = f32[16,128]{1,0:T(8,128)S(1)} fusion(f32[16,128,2048]{2,1,0:T(8,128)} %get-tuple-element.13, f32[16,128]{1,0:T(8,128)S(1)} %get-tuple-element.12), kind=kLoop, calls=%fused_computation.6 | loop fusion | flops 8386560 | bytes 16793600 | tf_op jit(solution)/shard_map/reduce_sum | solution.py:36
  279.5 47.1 %all-gather.11.cloned.1.call-done = bf16[2048,1024]{1,0:T(8,128)(2,1)} async-done(((bf16[256,1024]{1,0:T(8,128)(2,1)}), bf16[2048,1024]{1,0:T(8,128)(2,1)}) %all-gather.11.cloned.1.call-update) | async-done | bytes 4194320 | tf_op jit(solution)/shard_map/all_gather | solution.py:100
  326.6 6.5 copy.30
  333.1 0.0 copy-start.6
  333.1 10.2 %fusion.40 = bf16[128,16,64]{0,2,1:T(8,128)(2,1)S(1)} fusion(bf16[2048,16,64]{0,2,1:T(8,128)(2,1)} %bitcast.82, f32[16,128,2048]{2,1,0:T(8,128)} %get-tuple-element.13, f32[16,128]{1,0:T(8,128)S(1)} %get-tuple-element.12, f32[128,16]{0,1:T(8,128)S(1)} %bitcast_add_fusion.1, f32[128,16]{0,1:T(8,128)S(1)} %multiply_bitcast_fusion.1), kind=kOutput, calls=%fused_computation.38 | convolution fusion | flops 545652736 | bytes 21258240 | tf_op jit(solution)/shard_map/hqk,khd->qhd/dot_general | solution.py:37
  343.3 0.0 copy-done.6
  343.3 2.6 fusion.49
  345.9 0.0 all-reduce.5.cloned.1.call-update
  346.0 2.8 fusion.30
  348.7 189.1 %all-reduce.5.cloned.1.call-done = (f32[1024,1024]{1,0:T(8,128)}, f32[1024,1024]{1,0:T(8,128)}) async-done(((f32[1024,1024]{1,0:T(8,128)}, f32[1024,1024]{1,0:T(8,128)}), (f32[1024,1024]{1,0:T(8,128)}, f32[1024,1024]{1,0:T(8,128)})) %all-reduce.5.cloned.1.call-update) | async-done | bytes 8388624 | tf_op jit(solution)/shard_map/psum | solution.py:109
  537.8 0.0 copy-start.1
  537.8 175.9 %all-reduce.6 = (bf16[1024,1024]{1,0:T(8,128)(2,1)}, bf16[1024,1024]{1,0:T(8,128)(2,1)}) all-reduce(f32[1024,1024]{1,0:T(8,128)} %get-tuple-element.4, f32[1024,1024]{1,0:T(8,128)} %get-tuple-element.5), channel_id=1, replica_groups=mesh['dp'=16,'ctx'=8] {'ctx'}, use_global_device_ids=true, to_apply=%region_8.0 | all-reduce | flops 2097152 | bytes 12582912 | tf_op jit(solution)/shard_map/psum | solution.py:109
  713.7 0.0 copy-done.1
  (7 shorter events, 0.1 us)
Async XLA Ops:
  7.2 172.9 %copy-start = (bf16[1024,1024]{1,0:T(8,128)(2,1)S(1)}, bf16[1024,1024]{1,0:T(8,128)(2,1)}, u32[]{:S(2)}) copy-start(bf16[1024,1024]{1,0:T(8,128)(2,1)} %param.21) | copy-start | bytes 6291460
  7.2 4.9 copy-start.3
  7.2 4.9 copy-start.8
  7.2 79.1 %all-gather.5.cloned.1.call-start = ((), (), s32[]{:S(2)}) async-start(), calls=%async_computation | async-start | bytes 4718592 | tf_op jit(solution)/shard_map/all_gather | solution.py:85
  12.0 146.6 %all-gather.7.cloned.1.call-start = ((), (), s32[]{:S(2)}) async-start(), calls=%async_computation.1 | async-start | bytes 4718592 | tf_op jit(solution)/shard_map/all_gather | solution.py:86
  15.2 239.2 %all-gather.9.cloned.1.call-start = ((), (), s32[]{:S(2)}) async-start(), calls=%async_computation.2 | async-start | bytes 4718592 | tf_op jit(solution)/shard_map/all_gather | solution.py:99
  165.1 16.7 %copy-start.9 = (f32[1024]{0:T(1024)S(1)}, f32[1024]{0:T(1024)}, u32[]{:S(2)}) copy-start(f32[1024]{0:T(1024)} %param.22) | copy-start | bytes 12292
  180.9 0.8 copy-start.5
  181.7 6.9 copy-start.2
  181.7 7.0 copy-start.7
  184.9 6.1 copy-start.4
  185.0 141.6 %all-gather.11.cloned.1.call-start = ((), (), s32[]{:S(2)}) async-start(), calls=%async_computation.3 | async-start | bytes 4718592 | tf_op jit(solution)/shard_map/all_gather | solution.py:100
  188.4 349.4 %all-reduce.5.cloned.1.call-start = ((), (), s32[]{:S(2)}) async-start(), calls=%async_computation.4 | async-start | bytes 16777216 | tf_op jit(solution)/shard_map/psum | solution.py:109
  333.1 10.2 %copy-start.6 = (bf16[1,128,1024]{2,1,0:T(8,128)(2,1)S(1)}, bf16[1,128,1024]{2,1,0:T(8,128)(2,1)}, u32[]{:S(2)}) copy-start(bf16[1,128,1024]{2,1,0:T(8,128)(2,1)} %param.29) | copy-start | bytes 786436
  537.8 175.9 %copy-start.1 = (bf16[1024,1024]{1,0:T(8,128)(2,1)S(1)}, bf16[1024,1024]{1,0:T(8,128)(2,1)}, u32[]{:S(2)}) copy-start(bf16[1024,1024]{1,0:T(8,128)(2,1)} %param.21) | copy-start | bytes 6291460
Sparse Core Ops, SparseCore 0:
  12.1 74.0 all-gather.4
  89.2 69.3 all-gather.6
  185.1 69.3 all-gather.8
  257.2 69.3 all-gather.10
  346.1 191.6 all-reduce.4
